TPU v7x, 32 devices: a whole 2x2x4 slice. The times are simulated.
32 devices in a mesh: grp: 2 (over y), src: 8 (over z, x), tgt: 2 (over core).
Axes of the slice: x: 2, y: 2, z: 4, core: 2. Of those that a mesh axis runs over, the one named last changes fastest.
Arguments:
- source_feat: float32 [256, 64, 128], P(('grp', 'src')), parts along dimension 0, may hold values from -1.2 to 1.2
- target_feat: float32 [32, 64, 128], P(('grp', 'src', 'tgt')), parts along dimension 0, may hold values from -1.2 to 1.2
- log_mass_src: float32 [256, 128], P(('grp', 'src')), parts along dimension 0, may hold values from -3 to 3
- log_mass_tgt: float32 [32, 128], P(('grp', 'src', 'tgt')), parts along dimension 0, may hold values from -3 to 3
- potential_tgt: float32 [32, 128], P(('grp', 'src', 'tgt')), parts along dimension 0, may hold values from -6 to 152
- support: int32 [256, 2, 8], P(('grp', 'src'), 'tgt'), parts along dimension 0, may hold values from 0 to 7, as said below
- counts: int32 [256, 2], P(('grp', 'src'), 'tgt'), parts along dimension 0, may hold values from 1 to 8, as said below
Outputs:
- potential_src: float32 [256, 128], P(('grp', 'src')), parts along dimension 0
- potential_new: float32 [32, 128], P(('grp', 'src', 'tgt')), parts along dimension 0
There are 2 independent parts, one for each index of `grp`. A program takes and returns all parts, laid end to end along the dimension named above; each array names one. Nothing has to cross between parts.
Inputs may be any that keep to these rules, and one draw needn't show every extreme that they name: `support`: within one list the first counts entries are distinct; unused entries are also valid indices and are ignored; every target block of a shard is named within the used entries of some source block row. `counts`: the source block rows of one index of src share a load level, so some devices use far more slots than others; some list is full in every draw.
All inputs are finite; a program needn't handle non-finite values.
Results may differ from a plain program's by a relative error of at most 0.000096.
Values sent between devices are 32-bit elements; how exact they have to be, the bound alone decides.
A program may use at most 64 MiB of HBM per device.

v0:
```python
import math
import jax
import jax.numpy as jnp
from jax import lax
from jax.sharding import PartitionSpec as P

entropic = 0.5
very_low = -1e30


def merged(part, axis, combine):
    gathered = jax.tree.map(lambda a: lax.all_gather(a, axis), part)

    def take(source):
        return jax.tree.map(lambda a: lax.dynamic_index_in_dim(a, source, 0, False), gathered)

    return lax.fori_loop(
        1, lax.axis_size(axis), lambda source, state: combine(state, take(source)), take(0)
    )


def cost_tiles(source_blk, source_sq, target_blk, target_sq):
    cross = jnp.einsum(
        "...fi,...fj->...ij", source_blk, target_blk, precision=lax.Precision.HIGHEST
    )
    return source_sq[..., :, None] + target_sq[..., None, :] - 2.0 * cross


def row_stats(cost, mass_tgt, poten_tgt, usable):
    scores = mass_tgt[..., None, :] + (poten_tgt[..., None, :] - cost) / entropic
    scores = jnp.where(usable[..., None, None], scores, very_low)
    peak = jnp.max(scores, axis=(1, 3))
    total = jnp.sum(jnp.exp(scores - peak[:, None, :, None]), axis=(1, 3))
    return (peak, total)


def column_stats(cost, mass_src, poten_src, usable):
    scores = mass_src[:, None, :, None] + (poten_src[:, None, :, None] - cost) / entropic
    peak = jnp.max(scores, axis=2)
    total = jnp.sum(jnp.exp(scores - peak[:, :, None, :]), axis=2)
    peak = jnp.where(usable[..., None], peak, very_low)
    total = jnp.where(usable[..., None], total, 0.0)
    return (peak, total)


def merge_pair(first_pair, second_pair):
    first_peak, first_total = first_pair
    second_peak, second_total = second_pair
    highest = jnp.maximum(first_peak, second_peak)
    summed = first_total * jnp.exp(first_peak - highest) + second_total * jnp.exp(
        second_peak - highest
    )
    return (highest, summed)


def segment_merge(peaks, totals, seg_ids, segments):
    best = jax.ops.segment_max(peaks, seg_ids, num_segments=segments + 1)
    best = jnp.maximum(best, very_low)
    summed = jax.ops.segment_sum(
        totals * jnp.exp(peaks - best[seg_ids]), seg_ids, num_segments=segments + 1
    )
    return (best[:segments], summed[:segments])


def per_device(
    source_feat, target_feat, log_mass_src, log_mass_tgt, potential_tgt, support, counts
):
    target_all, mass_all, poten_all = (
        lax.all_gather(target_feat, "src", axis=0, tiled=True),
        lax.all_gather(log_mass_tgt, "src", axis=0, tiled=True),
        lax.all_gather(potential_tgt, "src", axis=0, tiled=True),
    )
    blocks = target_all.shape[0]
    rows_here = source_feat.shape[0]
    slots_here = support.shape[2]
    cells = source_feat.shape[2]
    indices = support[:, 0, :]
    limits = counts[:, 0]
    usable = jnp.arange(slots_here, dtype=jnp.int32)[None, :] < limits[:, None]
    source_sq = jnp.sum(source_feat * source_feat, axis=1)
    target_sq = jnp.sum(target_all * target_all, axis=1)
    width = math.gcd(rows_here, 4)

    def grouped(array):
        return array.reshape((rows_here // width, width) + array.shape[1:])

    def row_pass(items):
        source_blk, source_nrm, ids_here, use_here = items
        cost = cost_tiles(
            source_blk[:, None], source_nrm[:, None], target_all[ids_here], target_sq[ids_here]
        )
        return row_stats(cost, mass_all[ids_here], poten_all[ids_here], use_here)

    peak, total = lax.map(
        row_pass, (grouped(source_feat), grouped(source_sq), grouped(indices), grouped(usable))
    )
    peak = peak.reshape(rows_here, cells)
    total = total.reshape(rows_here, cells)
    peak_all, total_all = merged((peak, total), "tgt", merge_pair)
    potential_src = -entropic * (peak_all + jnp.log(total_all))

    def column_pass(items):
        source_blk, source_nrm, mass_here, poten_here, ids_here, use_here = items
        cost = cost_tiles(
            source_blk[:, None], source_nrm[:, None], target_all[ids_here], target_sq[ids_here]
        )
        return column_stats(cost, mass_here, poten_here, use_here)

    peaks, totals = lax.map(
        column_pass,
        (
            grouped(source_feat),
            grouped(source_sq),
            grouped(log_mass_src),
            grouped(potential_src),
            grouped(indices),
            grouped(usable),
        ),
    )
    seg_ids = jnp.where(usable, indices, blocks).reshape(-1)
    best, summed = segment_merge(
        peaks.reshape(-1, cells), totals.reshape(-1, cells), seg_ids, blocks
    )
    share = blocks // lax.axis_size("src")
    own_start = lax.axis_index("src") * share
    highest = lax.pmax(best, "src")
    whole = lax.psum(summed * jnp.exp(best - highest), "src")
    own_peak = lax.dynamic_slice_in_dim(highest, own_start, share, 0)
    own_total = lax.dynamic_slice_in_dim(whole, own_start, share, 0)
    potential_new = -entropic * (own_peak + jnp.log(own_total))
    return (potential_src, potential_new)


def solution(mesh):
    in_specs = (
        P(("grp", "src"), None, None),
        P(("grp", "src", "tgt"), None, None),
        P(("grp", "src"), None),
        P(("grp", "src", "tgt"), None),
        P(("grp", "src", "tgt"), None),
        P(("grp", "src"), "tgt", None),
        P(("grp", "src"), "tgt"),
    )
    out_specs = (P(("grp", "src"), None), P(("grp", "src", "tgt"), None))
    return jax.shard_map(
        per_device, mesh=mesh, in_specs=in_specs, out_specs=out_specs, check_vma=False
    )
```

profile of v0, /device:TPU:0, one launch (start us, length us, event | category | flops | bytes accessed | tf_op | source)
XLA Modules:
  0.0 177.5 jit_solution(18147925197401593971)
XLA Ops:
  1.2 1.3 reduce.3
  2.6 0.8 copy.19
  3.4 22.4 %all-gather = f32[8,1,128]{2,1,0:T(1,128)S(1)} all-gather(f32[1,1,128]{2,1,0:T(1,128)} %bitcast.189), channel_id=1, replica_groups=mesh['grp'=2,'src'=8,'tgt'=2] {'src'}, dimensions={0}, use_global_device_ids=true | all-gather | bytes 4608 | tf_op jit(solution)/shard_map/all_gather | solution.py:70
  25.8 16.5 %all-gather.1 = f32[8,1,128]{2,1,0:T(1,128)S(1)} all-gather(f32[1,1,128]{2,1,0:T(1,128)} %bitcast.190), channel_id=1, replica_groups=mesh['grp'=2,'src'=8,'tgt'=2] {'src'}, dimensions={0}, use_global_device_ids=true | all-gather | bytes 4608 | tf_op jit(solution)/shard_map/all_gather | solution.py:71
  42.3 1.1 multiply_reduce_fusion
  43.4 31.0 %all_gather.17 = f32[8,64,128]{2,1,0:T(8,128)S(1)} all-gather(f32[1,64,128]{2,1,0:T(8,128)} %param.12), channel_id=1, replica_groups=mesh['grp'=2,'src'=8,'tgt'=2] {'src'}, dimensions={0}, use_global_device_ids=true | all-gather | bytes 294912 | tf_op jit(solution)/shard_map/all_gather | solution.py:69
  74.5 35.7 %while.8 = (s32[]{:T(128)}, f32[4,4,128]{2,1,0:T(4,128)S(1)}, f32[4,4,128]{2,1,0:T(4,128)S(1)}, pred[4,4,8]{2,1,0:T(4,128)(4,1)S(1)}, s32[4,4,8]{2,1,0:T(4,128)S...) while((s32[]{:T(128)}, f32[4,4,128]{2,1,0:T(4,128)S(1)}, ...), condition=%wide.region_5.6_spmd, body=%wide.region_2.5_spmd.sunk | while | flops 407896160 | bytes 7644529 | solution.py:94
  74.6 0.6 gather_fusion
  77.0 6.1 %fusion.44 = (f32[4,128]{1,0:T(4,128)S(1)}, f32[4,8,128,128]{2,3,1,0:T(8,128)S(1)}) fusion(f32[4,8,64,128]{3,2,1,0:T(8,128)S(1)} %bitcast.172, f32[4,4,64,128]{3,2,1,0:T(8,128)} %get-tuple-element.388, s32[]{:T(128)S(6)} %copy.30, f32[4,8,128]{2,1,0:T(8,128)S(1)} %bitcast.175, f32[4,128]{1,0:T(4,128)S(1)} %dynamic-slice_bitcast_fusion.9, ...), kind=kOutput, calls=%fused_computation.75.clone.1 | convolution fusion | flops 406846976 | bytes 3330084 | tf_op jit(solution)/shard_map/while/body/eval_jaxpr/...fi,...fj->...ij/dot_general | solution.py:23
  85.9 6.1 %fusion.44 = (f32[4,128]{1,0:T(4,128)S(1)}, f32[4,8,128,128]{2,3,1,0:T(8,128)S(1)}) fusion(f32[4,8,64,128]{3,2,1,0:T(8,128)S(1)} %bitcast.172, f32[4,4,64,128]{3,2,1,0:T(8,128)} %get-tuple-element.388, s32[]{:T(128)S(6)} %copy.30, f32[4,8,128]{2,1,0:T(8,128)S(1)} %bitcast.175, f32[4,128]{1,0:T(4,128)S(1)} %dynamic-slice_bitcast_fusion.9, ...), kind=kOutput, calls=%fused_computation.75.clone.1 | convolution fusion | flops 406846976 | bytes 3330084 | tf_op jit(solution)/shard_map/while/body/eval_jaxpr/...fi,...fj->...ij/dot_general | solution.py:23
  94.8 6.1 %fusion.44 = (f32[4,128]{1,0:T(4,128)S(1)}, f32[4,8,128,128]{2,3,1,0:T(8,128)S(1)}) fusion(f32[4,8,64,128]{3,2,1,0:T(8,128)S(1)} %bitcast.172, f32[4,4,64,128]{3,2,1,0:T(8,128)} %get-tuple-element.388, s32[]{:T(128)S(6)} %copy.30, f32[4,8,128]{2,1,0:T(8,128)S(1)} %bitcast.175, f32[4,128]{1,0:T(4,128)S(1)} %dynamic-slice_bitcast_fusion.9, ...), kind=kOutput, calls=%fused_computation.75.clone.1 | convolution fusion | flops 406846976 | bytes 3330084 | tf_op jit(solution)/shard_map/while/body/eval_jaxpr/...fi,...fj->...ij/dot_general | solution.py:23
  103.8 6.1 %fusion.44 = (f32[4,128]{1,0:T(4,128)S(1)}, f32[4,8,128,128]{2,3,1,0:T(8,128)S(1)}) fusion(f32[4,8,64,128]{3,2,1,0:T(8,128)S(1)} %bitcast.172, f32[4,4,64,128]{3,2,1,0:T(8,128)} %get-tuple-element.388, s32[]{:T(128)S(6)} %copy.30, f32[4,8,128]{2,1,0:T(8,128)S(1)} %bitcast.175, f32[4,128]{1,0:T(4,128)S(1)} %dynamic-slice_bitcast_fusion.9, ...), kind=kOutput, calls=%fused_computation.75.clone.1 | convolution fusion | flops 406846976 | bytes 3330084 | tf_op jit(solution)/shard_map/while/body/eval_jaxpr/...fi,...fj->...ij/dot_general | solution.py:23
  110.2 1.8 %all_gather.19 = f32[2,16,128]{2,1,0:T(8,128)S(1)} all-gather(f32[1,16,128]{2,1,0:T(8,128)S(1)} %bitcast.188), channel_id=1, replica_groups=mesh['grp'=2,'src'=8,'tgt'=2] {'tgt'}, dimensions={0}, use_global_device_ids=true | all-gather | bytes 24576 | tf_op jit(solution)/shard_map/all_gather | solution.py:12
  112.0 1.8 %all_gather.18 = f32[2,16,128]{2,1,0:T(8,128)S(1)} all-gather(f32[1,16,128]{2,1,0:T(8,128)S(1)} %bitcast.187), channel_id=1, replica_groups=mesh['grp'=2,'src'=8,'tgt'=2] {'tgt'}, dimensions={0}, use_global_device_ids=true | all-gather | bytes 24576 | tf_op jit(solution)/shard_map/all_gather | solution.py:12
  113.9 0.6 fusion.19
  114.8 22.8 %while.9 = (s32[]{:T(128)}, f32[4,4,8,128]{3,2,1,0:T(8,128)S(1)}, f32[4,4,8,128]{3,2,1,0:T(8,128)S(1)}, pred[4,4,8]{2,1,0:T(4,128)(4,1)S(1)}, f32[4,4,128]{2,1,0...) while((s32[]{:T(128)}, f32[4,4,8,128]{3,2,1,0:T(8,128)S(1)}, ...), condition=%wide.region_9.10_spmd, body=%wide.region_6.9_spmd.sunk | while | flops 407372896 | bytes 7659093 | solution.py:109
  116.2 0.7 dynamic-slice_bitcast_fusion.12
  116.9 3.2 %fusion.46 = (f32[4,8,128]{2,1,0:T(8,128)S(1)}, f32[4,8,128,128]{3,2,1,0:T(8,128)S(1)}) fusion(f32[4,8,64,128]{3,2,1,0:T(8,128)S(1)} %bitcast.171, f32[4,4,64,128]{3,2,1,0:T(8,128)} %get-tuple-element.424, s32[]{:T(128)S(6)} %copy.39, f32[4,8,128]{2,1,0:T(8,128)S(1)} %bitcast.174, f32[4,128]{1,0:T(4,128)S(1)} %get-tuple-element.348, ...), kind=kOutput, calls=%fused_computation.76.clone.1 | convolution fusion | flops 406319104 | bytes 3315716 | tf_op jit(solution)/shard_map/while/body/eval_jaxpr/...fi,...fj->...ij/dot_general | solution.py:23
  120.6 0.6 gather_fusion.4
  121.9 0.7 dynamic-slice_bitcast_fusion.12
  122.5 3.2 %fusion.46 = (f32[4,8,128]{2,1,0:T(8,128)S(1)}, f32[4,8,128,128]{3,2,1,0:T(8,128)S(1)}) fusion(f32[4,8,64,128]{3,2,1,0:T(8,128)S(1)} %bitcast.171, f32[4,4,64,128]{3,2,1,0:T(8,128)} %get-tuple-element.424, s32[]{:T(128)S(6)} %copy.39, f32[4,8,128]{2,1,0:T(8,128)S(1)} %bitcast.174, f32[4,128]{1,0:T(4,128)S(1)} %get-tuple-element.348, ...), kind=kOutput, calls=%fused_computation.76.clone.1 | convolution fusion | flops 406319104 | bytes 3315716 | tf_op jit(solution)/shard_map/while/body/eval_jaxpr/...fi,...fj->...ij/dot_general | solution.py:23
  126.3 0.6 gather_fusion.4
  127.6 0.7 dynamic-slice_bitcast_fusion.12
  128.2 3.2 %fusion.46 = (f32[4,8,128]{2,1,0:T(8,128)S(1)}, f32[4,8,128,128]{3,2,1,0:T(8,128)S(1)}) fusion(f32[4,8,64,128]{3,2,1,0:T(8,128)S(1)} %bitcast.171, f32[4,4,64,128]{3,2,1,0:T(8,128)} %get-tuple-element.424, s32[]{:T(128)S(6)} %copy.39, f32[4,8,128]{2,1,0:T(8,128)S(1)} %bitcast.174, f32[4,128]{1,0:T(4,128)S(1)} %get-tuple-element.348, ...), kind=kOutput, calls=%fused_computation.76.clone.1 | convolution fusion | flops 406319104 | bytes 3315716 | tf_op jit(solution)/shard_map/while/body/eval_jaxpr/...fi,...fj->...ij/dot_general | solution.py:23
  132.0 0.6 gather_fusion.4
  133.3 0.7 dynamic-slice_bitcast_fusion.12
  133.9 3.2 %fusion.46 = (f32[4,8,128]{2,1,0:T(8,128)S(1)}, f32[4,8,128,128]{3,2,1,0:T(8,128)S(1)}) fusion(f32[4,8,64,128]{3,2,1,0:T(8,128)S(1)} %bitcast.171, f32[4,4,64,128]{3,2,1,0:T(8,128)} %get-tuple-element.424, s32[]{:T(128)S(6)} %copy.39, f32[4,8,128]{2,1,0:T(8,128)S(1)} %bitcast.174, f32[4,128]{1,0:T(4,128)S(1)} %get-tuple-element.348, ...), kind=kOutput, calls=%fused_computation.76.clone.1 | convolution fusion | flops 406319104 | bytes 3315716 | tf_op jit(solution)/shard_map/while/body/eval_jaxpr/...fi,...fj->...ij/dot_general | solution.py:23
  137.6 1.2 scatter_custom_fusion
  138.9 0.6 gather_fusion.6
  139.5 1.2 scatter_custom_fusion.1
  140.7 18.8 %pmax.7 = f32[8,128]{1,0:T(8,128)S(1)} all-reduce(f32[8,128]{1,0:T(8,128)S(1)} %slice.26), channel_id=1, replica_groups=mesh['grp'=2,'src'=8,'tgt'=2] {'src'}, use_global_device_ids=true, to_apply=%region_11.12 | all-reduce | flops 1024 | bytes 8192 | tf_op jit(solution)/shard_map/pmax | solution.py:126
  159.5 17.5 %psum.7 = f32[8,128]{1,0:T(8,128)S(1)} all-reduce(f32[8,128]{1,0:T(8,128)S(1)} %slice_multiply_fusion), channel_id=1, replica_groups=mesh['grp'=2,'src'=8,'tgt'=2] {'src'}, use_global_device_ids=true, to_apply=%region_13.14 | all-reduce | flops 1024 | bytes 8192 | tf_op jit(solution)/shard_map/psum | solution.py:127
  (99 shorter events, 17.2 us)
Async XLA Ops:
  74.5 40.0 %copy-start = (s32[16,1]{0,1:T(1,128)S(1)}, s32[16,1]{0,1:T(1,128)}, u32[]{:S(2)}) copy-start(s32[16,1]{0,1:T(1,128)} %param.17) | copy-start | bytes 196
where the time goes:
time: 178 us
  blocking collectives  110 us (62%)
  matrix products  37.3 us (21%)
  local copies, waits for them, and re-layouts  19.9 us (11%)
  other arithmetic  9.29 us (5%)
    dot_general x8, matrix products, cost_tiles(): jnp.einsum('...fi,...fj->...ij', source_blk, target_blk, precision=lax.Pr...  37.3 us
    all_gather x1, blocking collectives, per_device(): lax.all_gather(target_feat, 'src', axis=0, tiled=True)  31 us
    all_gather x1, blocking collectives, per_device(): lax.all_gather(log_mass_tgt, 'src', axis=0, tiled=True)  22.4 us
    pmax x1, blocking collectives, per_device(): highest = lax.pmax(best, 'src')  18.8 us
    psum x1, blocking collectives, per_device(): whole = lax.psum(summed * jnp.exp(best - highest), 'src')  17.5 us
    all_gather x1, blocking collectives, per_device(): lax.all_gather(potential_tgt, 'src', axis=0, tiled=True)  16.5 us
    gather x8, local copies, waits for them, and re-layouts, row_pass(): return row_stats(cost, mass_all[ids_here], poten_all[ids_here], use_here)  4.59 us
    all_gather x2, blocking collectives, merged(): gathered = jax.tree.map(lambda a: lax.all_gather(a, axis), part)  3.63 us

commit v1 on v0

--- a/solution.py
+++ b/solution.py
@@ -6,6 +6,12 @@
 
 entropic = 0.5
 very_low = -1e30
+
+
+def add_all(value, name):
+    parts = lax.all_gather(value, name, axis=0, tiled=False)
+    acc = parts.sum(axis=0)
+    return acc
 
 
 def merged(part, axis, combine):
@@ -124,7 +130,7 @@
     share = blocks // lax.axis_size("src")
     own_start = lax.axis_index("src") * share
     highest = lax.pmax(best, "src")
-    whole = lax.psum(summed * jnp.exp(best - highest), "src")
+    whole = add_all(summed * jnp.exp(best - highest), "src")
     own_peak = lax.dynamic_slice_in_dim(highest, own_start, share, 0)
     own_total = lax.dynamic_slice_in_dim(whole, own_start, share, 0)
     potential_new = -entropic * (own_peak + jnp.log(own_total))

time: 178 us -> 191 us (1.073)
  blocking collectives: 110 us -> 123 us
    all_gather x0 -> x1, blocking collectives: none -> 30.6 us  [add_all(): parts = lax.all_gather(value, name, axis=0, tiled=False)]
    psum x1 -> x0, blocking collectives: 17.5 us -> none  [per_device(): whole = lax.psum(summed * jnp.exp(best - highest), 'src')]
where the time goes in v1:
time: 191 us
  blocking collectives  123 us (64%)
  matrix products  37.3 us (20%)
  local copies, waits for them, and re-layouts  19.9 us (10%)
  other arithmetic  9.3 us (5%)
    dot_general x8, matrix products, cost_tiles(): jnp.einsum('...fi,...fj->...ij', source_blk, target_blk, precision=lax.Pr...  37.3 us
    all_gather x1, blocking collectives, per_device(): lax.all_gather(target_feat, 'src', axis=0, tiled=True)  31 us
    all_gather x1, blocking collectives, add_all(): parts = lax.all_gather(value, name, axis=0, tiled=False)  30.6 us
    all_gather x1, blocking collectives, per_device(): lax.all_gather(log_mass_tgt, 'src', axis=0, tiled=True)  22.4 us
    pmax x1, blocking collectives, per_device(): highest = lax.pmax(best, 'src')  18.8 us
    all_gather x1, blocking collectives, per_device(): lax.all_gather(potential_tgt, 'src', axis=0, tiled=True)  16.5 us
    gather x8, local copies, waits for them, and re-layouts, row_pass(): return row_stats(cost, mass_all[ids_here], poten_all[ids_here], use_here)  4.59 us

profile of v1, /device:TPU:0, one launch (start us, length us, event | category | flops | bytes accessed | tf_op | source)
XLA Modules:
  0.0 190.7 jit_solution(6817240457990687223)
XLA Ops:
  1.2 1.3 reduce.3
  2.6 0.8 copy.19
  3.4 22.4 %all-gather.1 = f32[8,1,128]{2,1,0:T(1,128)S(1)} all-gather(f32[1,1,128]{2,1,0:T(1,128)} %bitcast.191), channel_id=1, replica_groups=mesh['grp'=2,'src'=8,'tgt'=2] {'src'}, dimensions={0}, use_global_device_ids=true | all-gather | bytes 4608 | tf_op jit(solution)/shard_map/all_gather | solution.py:76
  25.8 16.5 %all-gather.2 = f32[8,1,128]{2,1,0:T(1,128)S(1)} all-gather(f32[1,1,128]{2,1,0:T(1,128)} %bitcast.192), channel_id=1, replica_groups=mesh['grp'=2,'src'=8,'tgt'=2] {'src'}, dimensions={0}, use_global_device_ids=true | all-gather | bytes 4608 | tf_op jit(solution)/shard_map/all_gather | solution.py:77
  42.3 1.1 multiply_reduce_fusion
  43.4 31.0 %all_gather.23 = f32[8,64,128]{2,1,0:T(8,128)S(1)} all-gather(f32[1,64,128]{2,1,0:T(8,128)} %param.12), channel_id=1, replica_groups=mesh['grp'=2,'src'=8,'tgt'=2] {'src'}, dimensions={0}, use_global_device_ids=true | all-gather | bytes 294912 | tf_op jit(solution)/shard_map/all_gather | solution.py:75
  74.5 35.7 %while.8 = (s32[]{:T(128)}, f32[4,4,128]{2,1,0:T(4,128)S(1)}, f32[4,4,128]{2,1,0:T(4,128)S(1)}, pred[4,4,8]{2,1,0:T(4,128)(4,1)S(1)}, s32[4,4,8]{2,1,0:T(4,128)S...) while((s32[]{:T(128)}, f32[4,4,128]{2,1,0:T(4,128)S(1)}, ...), condition=%wide.region_5.6_spmd, body=%wide.region_2.5_spmd.sunk | while | flops 407896160 | bytes 7644529 | solution.py:100
  74.6 0.6 gather_fusion
  77.0 6.1 %fusion.44 = (f32[4,128]{1,0:T(4,128)S(1)}, f32[4,8,128,128]{2,3,1,0:T(8,128)S(1)}) fusion(f32[4,8,64,128]{3,2,1,0:T(8,128)S(1)} %bitcast.174, f32[4,4,64,128]{3,2,1,0:T(8,128)} %get-tuple-element.388, s32[]{:T(128)S(6)} %copy.30, f32[4,8,128]{2,1,0:T(8,128)S(1)} %bitcast.177, f32[4,128]{1,0:T(4,128)S(1)} %dynamic-slice_bitcast_fusion.9, ...), kind=kOutput, calls=%fused_computation.76.clone.1 | convolution fusion | flops 406846976 | bytes 3330084 | tf_op jit(solution)/shard_map/while/body/eval_jaxpr/...fi,...fj->...ij/dot_general | solution.py:29
  85.9 6.1 %fusion.44 = (f32[4,128]{1,0:T(4,128)S(1)}, f32[4,8,128,128]{2,3,1,0:T(8,128)S(1)}) fusion(f32[4,8,64,128]{3,2,1,0:T(8,128)S(1)} %bitcast.174, f32[4,4,64,128]{3,2,1,0:T(8,128)} %get-tuple-element.388, s32[]{:T(128)S(6)} %copy.30, f32[4,8,128]{2,1,0:T(8,128)S(1)} %bitcast.177, f32[4,128]{1,0:T(4,128)S(1)} %dynamic-slice_bitcast_fusion.9, ...), kind=kOutput, calls=%fused_computation.76.clone.1 | convolution fusion | flops 406846976 | bytes 3330084 | tf_op jit(solution)/shard_map/while/body/eval_jaxpr/...fi,...fj->...ij/dot_general | solution.py:29
  94.8 6.1 %fusion.44 = (f32[4,128]{1,0:T(4,128)S(1)}, f32[4,8,128,128]{2,3,1,0:T(8,128)S(1)}) fusion(f32[4,8,64,128]{3,2,1,0:T(8,128)S(1)} %bitcast.174, f32[4,4,64,128]{3,2,1,0:T(8,128)} %get-tuple-element.388, s32[]{:T(128)S(6)} %copy.30, f32[4,8,128]{2,1,0:T(8,128)S(1)} %bitcast.177, f32[4,128]{1,0:T(4,128)S(1)} %dynamic-slice_bitcast_fusion.9, ...), kind=kOutput, calls=%fused_computation.76.clone.1 | convolution fusion | flops 406846976 | bytes 3330084 | tf_op jit(solution)/shard_map/while/body/eval_jaxpr/...fi,...fj->...ij/dot_general | solution.py:29
  103.8 6.1 %fusion.44 = (f32[4,128]{1,0:T(4,128)S(1)}, f32[4,8,128,128]{2,3,1,0:T(8,128)S(1)}) fusion(f32[4,8,64,128]{3,2,1,0:T(8,128)S(1)} %bitcast.174, f32[4,4,64,128]{3,2,1,0:T(8,128)} %get-tuple-element.388, s32[]{:T(128)S(6)} %copy.30, f32[4,8,128]{2,1,0:T(8,128)S(1)} %bitcast.177, f32[4,128]{1,0:T(4,128)S(1)} %dynamic-slice_bitcast_fusion.9, ...), kind=kOutput, calls=%fused_computation.76.clone.1 | convolution fusion | flops 406846976 | bytes 3330084 | tf_op jit(solution)/shard_map/while/body/eval_jaxpr/...fi,...fj->...ij/dot_general | solution.py:29
  110.2 1.8 all_gather.25
  112.0 1.8 all_gather.24
  113.9 0.6 fusion.19
  114.8 22.8 %while.9 = (s32[]{:T(128)}, f32[4,4,8,128]{3,2,1,0:T(8,128)S(1)}, f32[4,4,8,128]{3,2,1,0:T(8,128)S(1)}, pred[4,4,8]{2,1,0:T(4,128)(4,1)S(1)}, f32[4,4,128]{2,1,0...) while((s32[]{:T(128)}, f32[4,4,8,128]{3,2,1,0:T(8,128)S(1)}, ...), condition=%wide.region_9.10_spmd, body=%wide.region_6.9_spmd.sunk | while | flops 407372896 | bytes 7659093 | solution.py:115
  116.2 0.7 dynamic-slice_bitcast_fusion.12
  116.9 3.2 %fusion.46 = (f32[4,8,128]{2,1,0:T(8,128)S(1)}, f32[4,8,128,128]{3,2,1,0:T(8,128)S(1)}) fusion(f32[4,8,64,128]{3,2,1,0:T(8,128)S(1)} %bitcast.173, f32[4,4,64,128]{3,2,1,0:T(8,128)} %get-tuple-element.424, s32[]{:T(128)S(6)} %copy.39, f32[4,8,128]{2,1,0:T(8,128)S(1)} %bitcast.176, f32[4,128]{1,0:T(4,128)S(1)} %get-tuple-element.348, ...), kind=kOutput, calls=%fused_computation.77.clone.1 | convolution fusion | flops 406319104 | bytes 3315716 | tf_op jit(solution)/shard_map/while/body/eval_jaxpr/...fi,...fj->...ij/dot_general | solution.py:29
  120.6 0.6 gather_fusion.4
  121.9 0.7 dynamic-slice_bitcast_fusion.12
  122.5 3.2 %fusion.46 = (f32[4,8,128]{2,1,0:T(8,128)S(1)}, f32[4,8,128,128]{3,2,1,0:T(8,128)S(1)}) fusion(f32[4,8,64,128]{3,2,1,0:T(8,128)S(1)} %bitcast.173, f32[4,4,64,128]{3,2,1,0:T(8,128)} %get-tuple-element.424, s32[]{:T(128)S(6)} %copy.39, f32[4,8,128]{2,1,0:T(8,128)S(1)} %bitcast.176, f32[4,128]{1,0:T(4,128)S(1)} %get-tuple-element.348, ...), kind=kOutput, calls=%fused_computation.77.clone.1 | convolution fusion | flops 406319104 | bytes 3315716 | tf_op jit(solution)/shard_map/while/body/eval_jaxpr/...fi,...fj->...ij/dot_general | solution.py:29
  126.3 0.6 gather_fusion.4
  127.6 0.7 dynamic-slice_bitcast_fusion.12
  128.2 3.2 %fusion.46 = (f32[4,8,128]{2,1,0:T(8,128)S(1)}, f32[4,8,128,128]{3,2,1,0:T(8,128)S(1)}) fusion(f32[4,8,64,128]{3,2,1,0:T(8,128)S(1)} %bitcast.173, f32[4,4,64,128]{3,2,1,0:T(8,128)} %get-tuple-element.424, s32[]{:T(128)S(6)} %copy.39, f32[4,8,128]{2,1,0:T(8,128)S(1)} %bitcast.176, f32[4,128]{1,0:T(4,128)S(1)} %get-tuple-element.348, ...), kind=kOutput, calls=%fused_computation.77.clone.1 | convolution fusion | flops 406319104 | bytes 3315716 | tf_op jit(solution)/shard_map/while/body/eval_jaxpr/...fi,...fj->...ij/dot_general | solution.py:29
  132.0 0.6 gather_fusion.4
  133.3 0.7 dynamic-slice_bitcast_fusion.12
  133.9 3.2 %fusion.46 = (f32[4,8,128]{2,1,0:T(8,128)S(1)}, f32[4,8,128,128]{3,2,1,0:T(8,128)S(1)}) fusion(f32[4,8,64,128]{3,2,1,0:T(8,128)S(1)} %bitcast.173, f32[4,4,64,128]{3,2,1,0:T(8,128)} %get-tuple-element.424, s32[]{:T(128)S(6)} %copy.39, f32[4,8,128]{2,1,0:T(8,128)S(1)} %bitcast.176, f32[4,128]{1,0:T(4,128)S(1)} %get-tuple-element.348, ...), kind=kOutput, calls=%fused_computation.77.clone.1 | convolution fusion | flops 406319104 | bytes 3315716 | tf_op jit(solution)/shard_map/while/body/eval_jaxpr/...fi,...fj->...ij/dot_general | solution.py:29
  137.6 1.2 scatter_custom_fusion
  138.9 0.6 gather_fusion.6
  139.5 1.2 scatter_custom_fusion.1
  140.7 18.8 %pmax.7 = f32[8,128]{1,0:T(8,128)S(1)} all-reduce(f32[8,128]{1,0:T(8,128)S(1)} %slice.26), channel_id=1, replica_groups=mesh['grp'=2,'src'=8,'tgt'=2] {'src'}, use_global_device_ids=true, to_apply=%region_11.12 | all-reduce | flops 1024 | bytes 8192 | tf_op jit(solution)/shard_map/pmax | solution.py:132
  159.5 30.6 %all-gather = f32[64,128]{1,0:T(8,128)S(1)} all-gather(f32[8,128]{1,0:T(8,128)S(1)} %slice_multiply_fusion), channel_id=2, replica_groups=mesh['grp'=2,'src'=8,'tgt'=2] {'src'}, dimensions={0}, use_global_device_ids=true | all-gather | bytes 36864 | tf_op jit(solution)/shard_map/all_gather | solution.py:12
  (100 shorter events, 17.2 us)
Async XLA Ops:
  74.5 40.0 %copy-start = (s32[16,1]{0,1:T(1,128)S(1)}, s32[16,1]{0,1:T(1,128)}, u32[]{:S(2)}) copy-start(s32[16,1]{0,1:T(1,128)} %param.17) | copy-start | bytes 196
